TPU v7x, 32 devices: a whole 2x2x4 slice. The times are simulated.
32 devices in a mesh: section: 2 (over core), seq: 4 (over y, x), tensor: 4 (over z).
Axes of the slice: x: 2, y: 2, z: 4, core: 2. Of those that a mesh axis runs over, the one named last changes fastest.
Arguments:
- tokens: bfloat16 [4096, 1024], P('seq', 'tensor'), may hold values from -6 to 6
- segments: int32 [8, 512], P('seq'), may hold values from 0 to 3, never falling along the last dimension, each value on 1 to 256 neighbouring positions
- cotangent: bfloat16 [4096, 1024], P('seq', 'tensor'), may hold values from -6 to 6
- norm1_gain: bfloat16 [2, 1024], P('section', ('tensor', 'seq')), may hold values from 0.5 to 1.5
- norm1_bias: bfloat16 [2, 1024], P('section', ('tensor', 'seq')), may hold values from -3 to 3
- qkv_weight: bfloat16 [2, 1024, 16, 192], P('section', 'seq', 'tensor'), may hold values from -0.1875 to 0.1875
- qv_bias: bfloat16 [2, 16, 128], P('section', 'tensor', 'seq'), may hold values from -4 to 4
- out_weight: bfloat16 [2, 16, 64, 1024], P('section', 'tensor', None, 'seq'), may hold values from -0.75 to 0.75
- out_bias: bfloat16 [2, 1024], P('section', ('tensor', 'seq')), may hold values from -3 to 3
- norm2_gain: bfloat16 [2, 1024], P('section', ('tensor', 'seq')), may hold values from 0.5 to 1.5
- norm2_bias: bfloat16 [2, 1024], P('section', ('tensor', 'seq')), may hold values from -3 to 3
- up_weight: bfloat16 [2, 1024, 4096], P('section', 'seq', 'tensor'), may hold values from -0.1875 to 0.1875
- up_bias: bfloat16 [2, 4096], P('section', ('tensor', 'seq')), may hold values from -4 to 4
- down_weight: bfloat16 [2, 4096, 1024], P('section', 'tensor', 'seq'), may hold values from -0.09375 to 0.09375
- down_bias: bfloat16 [2, 1024], P('section', ('tensor', 'seq')), may hold values from -3 to 3
Outputs:
- section_out: bfloat16 [2, 4096, 1024], P('section', 'seq', 'tensor')
- input_grad: bfloat16 [2, 4096, 1024], P('section', 'seq', 'tensor')
- grad_norm1_gain: float32 [2, 1024], P('section', ('tensor', 'seq'))
- grad_norm1_bias: float32 [2, 1024], P('section', ('tensor', 'seq'))
- grad_qkv_weight: float32 [2, 1024, 16, 192], P('section', 'seq', 'tensor')
- grad_qv_bias: float32 [2, 16, 128], P('section', 'tensor', 'seq')
- grad_out_weight: float32 [2, 16, 64, 1024], P('section', 'tensor', None, 'seq')
- grad_out_bias: float32 [2, 1024], P('section', ('tensor', 'seq'))
- grad_norm2_gain: float32 [2, 1024], P('section', ('tensor', 'seq'))
- grad_norm2_bias: float32 [2, 1024], P('section', ('tensor', 'seq'))
- grad_up_weight: float32 [2, 1024, 4096], P('section', 'seq', 'tensor')
- grad_up_bias: float32 [2, 4096], P('section', ('tensor', 'seq'))
- grad_down_weight: float32 [2, 4096, 1024], P('section', 'tensor', 'seq')
- grad_down_bias: float32 [2, 1024], P('section', ('tensor', 'seq'))
Inputs may be any that keep to these rules, and one draw needn't show every extreme that they name: `segments`: along each sequence the document numbers never fall; every document holds 1 to 256 positions.
All inputs are finite; a program needn't handle non-finite values.
Results may differ from a plain program's by a relative error of at most 0.02.
Values may be sent and summed in bfloat16 or wider, within the bound.
A program may use at most 192 MiB of HBM per device.

v0:
```python
import math
import jax
import jax.numpy as jnp
from jax import lax
from jax.sharding import PartitionSpec as P

D = 1024
MB = 2
epsilon = 1e-05
floor_value = -1e30


def passed_along(shard, axis, by):
    devices = lax.axis_size(axis)
    pairs = [(i, i + by) for i in range(devices) if 0 <= i + by < devices]
    return lax.ppermute(shard, axis, pairs)


def row_totals(first, second):
    return lax.psum((jnp.sum(first, axis=1), jnp.sum(second, axis=1)), "tensor")


def norm_forward(rows, gain, shift):
    total, square = row_totals(rows, rows * rows)
    average = total / D
    variance = square / D - average * average
    scale = lax.rsqrt(variance + epsilon)
    centred = (rows - average[:, None]) * scale[:, None]
    return (centred, scale, centred * gain + shift)


def norm_backward(grad, centred, scale, gain):
    scaled = grad * gain
    total, along = row_totals(scaled, scaled * centred)
    return scale[:, None] * (scaled - total[:, None] / D - centred * along[:, None] / D)


def full_rows(piece):
    return lax.all_gather(piece, "tensor", axis=1, tiled=True)


def head_sums(partial_rows):
    return lax.psum_scatter(
        partial_rows.astype(jnp.bfloat16), "tensor", scatter_dimension=1, tiled=True
    ).astype(jnp.float32)


def grad_full(piece):
    return lax.all_gather(piece, "tensor", axis=1, tiled=True)


def back_sums(partial_rows):
    return lax.psum_scatter(
        partial_rows.astype(jnp.bfloat16), "tensor", scatter_dimension=1, tiled=True
    ).astype(jnp.float32)


def allowed_mask(segment):
    length = segment.shape[1]
    place = lax.broadcasted_iota(jnp.int32, (length, length), 0)
    other = lax.broadcasted_iota(jnp.int32, (length, length), 1)
    same = segment[:, :, None] == segment[:, None, :]
    return (same & (other <= place)[None])[:, None]


def attention_scores(query, keys, segment):
    head_dim = query.shape[-1]
    factor = 1.0 / math.sqrt(head_dim)
    scores = jnp.einsum("sqhe,skhe->shqk", query, keys, preferred_element_type=jnp.float32) * factor
    return (jnp.where(allowed_mask(segment), scores, floor_value), factor)


def forward(rows, segment, weights):
    gain1, bias1, w_qkv, b_qv, w_out, b_out, gain2, bias2, w_up, b_up, w_down, b_down = weights
    count_rows = rows.shape[0]
    heads = w_qkv.shape[1]
    head_dim = w_qkv.shape[2] // 3
    shape4 = (segment.shape[0], segment.shape[1], heads, head_dim)
    centred1, scale1, normed1 = norm_forward(rows, gain1, bias1)
    normed_whole = full_rows(normed1.astype(jnp.bfloat16))
    mixed = jnp.einsum("rd,dhe->rhe", normed_whole, w_qkv, preferred_element_type=jnp.float32)
    query = (mixed[..., :head_dim] + b_qv[:, :head_dim]).astype(jnp.bfloat16).reshape(shape4)
    keys = mixed[..., head_dim : 2 * head_dim].astype(jnp.bfloat16).reshape(shape4)
    values = (mixed[..., 2 * head_dim :] + b_qv[:, head_dim:]).astype(jnp.bfloat16).reshape(shape4)
    masked, factor = attention_scores(query, keys, segment)
    highest_score = jnp.max(masked, axis=-1, keepdims=True)
    raised = jnp.exp(masked - highest_score)
    total = jnp.sum(raised, axis=-1, keepdims=True)
    chance = (raised / total).astype(jnp.bfloat16)
    logsum = highest_score + jnp.log(total)
    context = jnp.einsum("shqk,skhe->sqhe", chance, values, preferred_element_type=jnp.float32)
    context = context.reshape(count_rows, heads * head_dim).astype(jnp.bfloat16)
    attn_part = jnp.dot(
        context, w_out.reshape(heads * head_dim, w_out.shape[2]), preferred_element_type=jnp.float32
    )
    hidden = rows + (head_sums(attn_part) + b_out)
    centred2, scale2, normed2 = norm_forward(hidden, gain2, bias2)
    normed2_whole = full_rows(normed2.astype(jnp.bfloat16))
    upper = jnp.dot(normed2_whole, w_up, preferred_element_type=jnp.float32) + b_up
    active = jax.nn.gelu(upper, approximate=True).astype(jnp.bfloat16)
    branch = head_sums(jnp.dot(active, w_down, preferred_element_type=jnp.float32)) + b_down
    output = (hidden + branch).astype(jnp.bfloat16)
    kept = (
        centred1,
        scale1,
        normed_whole,
        query,
        keys,
        values,
        logsum,
        context,
        centred2,
        scale2,
        normed2_whole,
        upper,
        active,
    )
    return (output, kept)


def gelu_value(upper):
    return jax.nn.gelu(upper, approximate=True)


def backward(grad_out, segment, weights, kept):
    gain1, bias1, w_qkv, b_qv, w_out, b_out, gain2, bias2, w_up, b_up, w_down, b_down = weights
    (
        centred1,
        scale1,
        normed_whole,
        query,
        keys,
        values,
        logsum,
        context,
        centred2,
        scale2,
        normed2_whole,
        upper,
        active,
    ) = kept
    count_rows = grad_out.shape[0]
    heads = w_qkv.shape[1]
    head_dim = w_qkv.shape[2] // 3
    shape4 = query.shape
    grad_branch = grad_out.astype(jnp.bfloat16)
    branch_whole = grad_full(grad_branch)
    grad_down = jnp.einsum("rf,rd->fd", active, branch_whole, preferred_element_type=jnp.float32)
    grad_active = jnp.einsum("rd,fd->rf", branch_whole, w_down, preferred_element_type=jnp.float32)
    grad_upper = jax.vjp(gelu_value, upper)[1](grad_active)[0].astype(jnp.bfloat16)
    grad_up = jnp.einsum("rd,rf->df", normed2_whole, grad_upper, preferred_element_type=jnp.float32)
    grad_normed2 = back_sums(
        jnp.einsum("rf,df->rd", grad_upper, w_up, preferred_element_type=jnp.float32)
    )
    grad_hidden = grad_out + norm_backward(grad_normed2, centred2, scale2, gain2)
    grad_attn = grad_hidden.astype(jnp.bfloat16)
    attn_whole = grad_full(grad_attn)
    out_matrix = w_out.reshape(heads * head_dim, w_out.shape[2])
    grad_out_w = jnp.einsum("rc,rd->cd", context, attn_whole, preferred_element_type=jnp.float32)
    grad_context = jnp.einsum(
        "rd,cd->rc", attn_whole, out_matrix, preferred_element_type=jnp.float32
    )
    grad_context = grad_context.astype(jnp.bfloat16).reshape(shape4)
    masked, factor = attention_scores(query, keys, segment)
    chance_full = jnp.exp(masked - logsum)
    chance = chance_full.astype(jnp.bfloat16)
    grad_chance = jnp.einsum(
        "sqhe,skhe->shqk", grad_context, values, preferred_element_type=jnp.float32
    )
    delta = jnp.sum(grad_chance * chance_full, axis=-1, keepdims=True)
    grad_scores = (chance_full * (grad_chance - delta)).astype(jnp.bfloat16)
    grad_query = (
        jnp.einsum("shqk,skhe->sqhe", grad_scores, keys, preferred_element_type=jnp.float32)
        * factor
    ).astype(jnp.bfloat16)
    grad_keys = (
        jnp.einsum("shqk,sqhe->skhe", grad_scores, query, preferred_element_type=jnp.float32)
        * factor
    ).astype(jnp.bfloat16)
    grad_values = jnp.einsum(
        "shqk,sqhe->skhe", chance, grad_context, preferred_element_type=jnp.float32
    ).astype(jnp.bfloat16)
    grad_mixed = jnp.concatenate([grad_query, grad_keys, grad_values], axis=-1).reshape(
        count_rows, heads, 3 * head_dim
    )
    grad_qkv = jnp.einsum(
        "rd,rhe->dhe", normed_whole, grad_mixed, preferred_element_type=jnp.float32
    )
    grad_qv = jnp.concatenate(
        [
            jnp.sum(grad_query.astype(jnp.float32), axis=(0, 1)),
            jnp.sum(grad_values.astype(jnp.float32), axis=(0, 1)),
        ],
        axis=-1,
    )
    grad_normed1 = back_sums(
        jnp.einsum("rhe,dhe->rd", grad_mixed, w_qkv, preferred_element_type=jnp.float32)
    )
    grad_rows_total = grad_hidden + norm_backward(grad_normed1, centred1, scale1, gain1)
    grads = (
        jnp.sum(grad_normed1 * centred1, axis=0),
        jnp.sum(grad_normed1, axis=0),
        grad_qkv,
        grad_qv,
        grad_out_w.reshape(w_out.shape),
        jnp.sum(grad_attn.astype(jnp.float32), axis=0),
        jnp.sum(grad_normed2 * centred2, axis=0),
        jnp.sum(grad_normed2, axis=0),
        grad_up,
        jnp.sum(grad_upper.astype(jnp.float32), axis=0),
        grad_down,
        jnp.sum(grad_branch.astype(jnp.float32), axis=0),
    )
    return (grad_rows_total.astype(jnp.bfloat16), grads)


def body(
    tokens,
    segments,
    cotangent,
    norm1_gain,
    norm1_bias,
    qkv_weight,
    qv_bias,
    out_weight,
    out_bias,
    norm2_gain,
    norm2_bias,
    up_weight,
    up_bias,
    down_weight,
    down_bias,
):
    section = lax.axis_index("section")
    first_section = section == 0
    gathered = (
        lax.all_gather(norm1_gain[0], "seq", axis=0, tiled=True),
        lax.all_gather(norm1_bias[0], "seq", axis=0, tiled=True),
        lax.all_gather(qkv_weight[0], "seq", axis=0, tiled=True),
        lax.all_gather(qv_bias[0], "seq", axis=1, tiled=True),
        lax.all_gather(out_weight[0], "seq", axis=2, tiled=True),
        lax.all_gather(out_bias[0], "seq", axis=0, tiled=True),
        lax.all_gather(norm2_gain[0], "seq", axis=0, tiled=True),
        lax.all_gather(norm2_bias[0], "seq", axis=0, tiled=True),
        lax.all_gather(up_weight[0], "seq", axis=0, tiled=True),
        lax.all_gather(up_bias[0], "seq", axis=0, tiled=True),
        lax.all_gather(down_weight[0], "seq", axis=1, tiled=True),
        lax.all_gather(down_bias[0], "seq", axis=0, tiled=True),
    )
    weights = (
        gathered[0].astype(jnp.float32),
        gathered[1].astype(jnp.float32),
        gathered[2],
        gathered[3].astype(jnp.float32),
        gathered[4],
        gathered[5].astype(jnp.float32),
        gathered[6].astype(jnp.float32),
        gathered[7].astype(jnp.float32),
        gathered[8],
        gathered[9].astype(jnp.float32),
        gathered[10],
        gathered[11].astype(jnp.float32),
    )
    rows_batch = tokens.shape[0] // MB
    seqs_batch = segments.shape[0] // MB
    width_local = tokens.shape[1]
    received = jnp.zeros((rows_batch, width_local), jnp.bfloat16)
    outputs = jnp.zeros(tokens.shape, jnp.bfloat16)
    stash = []
    for tick in range(MB + 1):
        own = min(tick, MB - 1)
        batch = tick - section
        valid = (batch >= 0) & (batch < MB)
        placed = jnp.clip(batch, 0, MB - 1)
        entry = jnp.where(
            first_section, tokens[own * rows_batch : (own + 1) * rows_batch], received
        )
        segment = lax.dynamic_slice_in_dim(segments, placed * seqs_batch, seqs_batch, 0)
        result, kept = forward(entry.astype(jnp.float32), segment, weights)
        stash.append((entry, segment))
        current = lax.dynamic_slice_in_dim(outputs, placed * rows_batch, rows_batch, 0)
        outputs = lax.dynamic_update_slice_in_dim(
            outputs, jnp.where(valid, result, current), placed * rows_batch, 0
        )
        if tick < MB:
            received = passed_along(result, "section", 1)
    totals = jax.tree.map(lambda item: jnp.zeros(item.shape, jnp.float32), gathered)
    returned = jnp.zeros((rows_batch, width_local), jnp.bfloat16)
    input_grads = jnp.zeros(tokens.shape, jnp.bfloat16)
    for tick in range(MB + 1):
        own = min(tick, MB - 1)
        batch = tick - (1 - section)
        valid = (batch >= 0) & (batch < MB)
        placed = jnp.clip(batch, 0, MB - 1)
        grad_in = jnp.where(
            first_section, returned, cotangent[own * rows_batch : (own + 1) * rows_batch]
        ).astype(jnp.float32)
        earlier = stash[max(tick - 1, 0)]
        later = stash[min(tick + 1, MB)]
        picked = jax.tree.map(
            lambda left, right: jnp.where(first_section, left, right), earlier, later
        )
        entry = picked[0]
        segment = picked[1]
        kept = forward(entry.astype(jnp.float32), segment, weights)[1]
        grad_rows_out, grads = backward(grad_in, segment, weights, kept)
        totals = jax.tree.map(lambda acc, new: acc + jnp.where(valid, new, 0.0), totals, grads)
        current = lax.dynamic_slice_in_dim(input_grads, placed * rows_batch, rows_batch, 0)
        input_grads = lax.dynamic_update_slice_in_dim(
            input_grads, jnp.where(valid, grad_rows_out, current), placed * rows_batch, 0
        )
        if tick < MB:
            returned = passed_along(grad_rows_out, "section", -1)
    reduced = (
        lax.psum_scatter(
            totals[0].astype(jnp.bfloat16), "seq", scatter_dimension=0, tiled=True
        ).astype(jnp.float32),
        lax.psum_scatter(
            totals[1].astype(jnp.bfloat16), "seq", scatter_dimension=0, tiled=True
        ).astype(jnp.float32),
        lax.psum_scatter(
            totals[2].astype(jnp.bfloat16), "seq", scatter_dimension=0, tiled=True
        ).astype(jnp.float32),
        lax.psum_scatter(
            totals[3].astype(jnp.bfloat16), "seq", scatter_dimension=1, tiled=True
        ).astype(jnp.float32),
        lax.psum_scatter(
            totals[4].astype(jnp.bfloat16), "seq", scatter_dimension=2, tiled=True
        ).astype(jnp.float32),
        lax.psum_scatter(
            totals[5].astype(jnp.bfloat16), "seq", scatter_dimension=0, tiled=True
        ).astype(jnp.float32),
        lax.psum_scatter(
            totals[6].astype(jnp.bfloat16), "seq", scatter_dimension=0, tiled=True
        ).astype(jnp.float32),
        lax.psum_scatter(
            totals[7].astype(jnp.bfloat16), "seq", scatter_dimension=0, tiled=True
        ).astype(jnp.float32),
        lax.psum_scatter(
            totals[8].astype(jnp.bfloat16), "seq", scatter_dimension=0, tiled=True
        ).astype(jnp.float32),
        lax.psum_scatter(
            totals[9].astype(jnp.bfloat16), "seq", scatter_dimension=0, tiled=True
        ).astype(jnp.float32),
        lax.psum_scatter(
            totals[10].astype(jnp.bfloat16), "seq", scatter_dimension=1, tiled=True
        ).astype(jnp.float32),
        lax.psum_scatter(
            totals[11].astype(jnp.bfloat16), "seq", scatter_dimension=0, tiled=True
        ).astype(jnp.float32),
    )
    return (outputs[None], input_grads[None]) + tuple((item[None] for item in reduced))


def solution(mesh):
    return jax.shard_map(
        body,
        mesh=mesh,
        in_specs=(
            P("seq", "tensor"),
            P("seq", None),
            P("seq", "tensor"),
            P("section", ("tensor", "seq")),
            P("section", ("tensor", "seq")),
            P("section", "seq", "tensor", None),
            P("section", "tensor", "seq"),
            P("section", "tensor", None, "seq"),
            P("section", ("tensor", "seq")),
            P("section", ("tensor", "seq")),
            P("section", ("tensor", "seq")),
            P("section", "seq", "tensor"),
            P("section", ("tensor", "seq")),
            P("section", "tensor", "seq"),
            P("section", ("tensor", "seq")),
        ),
        out_specs=(
            P("section", "seq", "tensor"),
            P("section", "seq", "tensor"),
            P("section", ("tensor", "seq")),
            P("section", ("tensor", "seq")),
            P("section", "seq", "tensor", None),
            P("section", "tensor", "seq"),
            P("section", "tensor", None, "seq"),
            P("section", ("tensor", "seq")),
            P("section", ("tensor", "seq")),
            P("section", ("tensor", "seq")),
            P("section", "seq", "tensor"),
            P("section", ("tensor", "seq")),
            P("section", "tensor", "seq"),
            P("section", ("tensor", "seq")),
        ),
        check_vma=False,
    )
```

profile of v0, /device:TPU:0, one launch (start us, length us, event | category | flops | bytes accessed | tf_op | source)
XLA Modules:
  0.0 1450.4 jit_solution(4128099430230138480)
XLA Ops:
  67.1 30.9 %all-gather.70.cloned.1.call-done = bf16[1,1024,4,192]{1,3,2,0:T(8,128)(2,1)} async-done(((bf16[1,256,4,192]{1,3,2,0:T(8,128)(2,1)}), bf16[1,1024,4,192]{1,3,2,0:T(8,128)(2,1)}) %all-gather.70.cloned.1.call-update) | async-done | bytes 1572880 | tf_op jit(solution)/shard_map/all_gather | solution.py:239
  109.8 26.2 %reduce-scatter.23.cloned.1.call-done = bf16[512,256]{1,0:T(8,128)(2,1)} async-done(((bf16[512,1024]{1,0:T(8,128)(2,1)}), bf16[512,256]{1,0:T(8,128)(2,1)}) %reduce-scatter.23.cloned.1.call-update) | async-done | bytes 262160 | tf_op jit(solution)/shard_map/reduce_scatter | solution.py:43
  171.2 36.9 %all-gather.72.cloned.1.call-done = bf16[1,1024,1024]{2,1,0:T(8,128)(2,1)} async-done(((bf16[1,256,1024]{2,1,0:T(8,128)(2,1)}), bf16[1,1024,1024]{2,1,0:T(8,128)(2,1)}) %all-gather.72.cloned.1.call-update) | async-done | bytes 2097168 | tf_op jit(solution)/shard_map/all_gather | solution.py:245
  208.1 31.9 %all-gather.36.cloned.1.call-done = bf16[512,1024]{1,0:T(8,128)(2,1)} async-done(((bf16[512,256]{1,0:T(8,128)(2,1)}), bf16[512,1024]{1,0:T(8,128)(2,1)}) %all-gather.36.cloned.1.call-update) | async-done | bytes 1048592 | tf_op jit(solution)/shard_map/all_gather | solution.py:39
  246.3 25.7 %reduce-scatter.25.cloned.1.call-done = bf16[512,256]{1,0:T(8,128)(2,1)} async-done(((bf16[512,1024]{1,0:T(8,128)(2,1)}), bf16[512,256]{1,0:T(8,128)(2,1)}) %reduce-scatter.25.cloned.1.call-update) | async-done | bytes 262160 | tf_op jit(solution)/shard_map/reduce_scatter | solution.py:43
  286.7 28.2 %all-gather.46.cloned.1.call-done = bf16[512,1024]{1,0:T(8,128)(2,1)} async-done(((bf16[512,256]{1,0:T(8,128)(2,1)}), bf16[512,1024]{1,0:T(8,128)(2,1)}) %all-gather.46.cloned.1.call-update) | async-done | bytes 1048592 | tf_op jit(solution)/shard_map/all_gather | solution.py:39
  323.9 25.5 %reduce-scatter.35.cloned.1.call-done = bf16[512,256]{1,0:T(8,128)(2,1)} async-done(((bf16[512,1024]{1,0:T(8,128)(2,1)}), bf16[512,256]{1,0:T(8,128)(2,1)}) %reduce-scatter.35.cloned.1.call-update) | async-done | bytes 262160 | tf_op jit(solution)/shard_map/reduce_scatter | solution.py:43
  364.5 25.2 %all-gather.38.cloned.1.call-done = bf16[512,1024]{1,0:T(8,128)(2,1)} async-done(((bf16[512,256]{1,0:T(8,128)(2,1)}), bf16[512,1024]{1,0:T(8,128)(2,1)}) %all-gather.38.cloned.1.call-update) | async-done | bytes 1048592 | tf_op jit(solution)/shard_map/all_gather | solution.py:39
  424.6 25.8 %all-gather.48.cloned.1.call-done = bf16[512,1024]{1,0:T(8,128)(2,1)} async-done(((bf16[512,256]{1,0:T(8,128)(2,1)}), bf16[512,1024]{1,0:T(8,128)(2,1)}) %all-gather.48.cloned.1.call-update) | async-done | bytes 1048592 | tf_op jit(solution)/shard_map/all_gather | solution.py:49
  478.9 28.6 %reduce-scatter.37.cloned.1.call-done = bf16[512,256]{1,0:T(8,128)(2,1)} async-done(((bf16[512,1024]{1,0:T(8,128)(2,1)}), bf16[512,256]{1,0:T(8,128)(2,1)}) %reduce-scatter.37.cloned.1.call-update) | async-done | bytes 262160 | tf_op jit(solution)/shard_map/reduce_scatter | solution.py:53
  520.8 28.8 %all-gather.40.cloned.1.call-done = bf16[512,1024]{1,0:T(8,128)(2,1)} async-done(((bf16[512,256]{1,0:T(8,128)(2,1)}), bf16[512,1024]{1,0:T(8,128)(2,1)}) %all-gather.40.cloned.1.call-update) | async-done | bytes 1048592 | tf_op jit(solution)/shard_map/all_gather | solution.py:39
  555.7 25.7 %reduce-scatter.29.cloned.1.call-done = bf16[512,256]{1,0:T(8,128)(2,1)} async-done(((bf16[512,1024]{1,0:T(8,128)(2,1)}), bf16[512,256]{1,0:T(8,128)(2,1)}) %reduce-scatter.29.cloned.1.call-update) | async-done | bytes 262160 | tf_op jit(solution)/shard_map/reduce_scatter | solution.py:43
  597.1 28.5 %all-gather.52.cloned.1.call-done = bf16[512,1024]{1,0:T(8,128)(2,1)} async-done(((bf16[512,256]{1,0:T(8,128)(2,1)}), bf16[512,1024]{1,0:T(8,128)(2,1)}) %all-gather.52.cloned.1.call-update) | async-done | bytes 1048592 | tf_op jit(solution)/shard_map/all_gather | solution.py:49
  637.4 25.7 %reduce-scatter.39.cloned.1.call-done = bf16[512,256]{1,0:T(8,128)(2,1)} async-done(((bf16[512,1024]{1,0:T(8,128)(2,1)}), bf16[512,256]{1,0:T(8,128)(2,1)}) %reduce-scatter.39.cloned.1.call-update) | async-done | bytes 262160 | tf_op jit(solution)/shard_map/reduce_scatter | solution.py:53
  666.0 28.4 %all-gather.54.cloned.1.call-done = bf16[512,1024]{1,0:T(8,128)(2,1)} async-done(((bf16[512,256]{1,0:T(8,128)(2,1)}), bf16[512,1024]{1,0:T(8,128)(2,1)}) %all-gather.54.cloned.1.call-update) | async-done | bytes 1048592 | tf_op jit(solution)/shard_map/all_gather | solution.py:39
  702.5 25.7 %reduce-scatter.41.cloned.1.call-done = bf16[512,256]{1,0:T(8,128)(2,1)} async-done(((bf16[512,1024]{1,0:T(8,128)(2,1)}), bf16[512,256]{1,0:T(8,128)(2,1)}) %reduce-scatter.41.cloned.1.call-update) | async-done | bytes 262160 | tf_op jit(solution)/shard_map/reduce_scatter | solution.py:43
  754.9 19.9 %all-gather.62.cloned.1.call-done = bf16[512,1024]{1,0:T(8,128)(2,1)} async-done(((bf16[512,256]{1,0:T(8,128)(2,1)}), bf16[512,1024]{1,0:T(8,128)(2,1)}) %all-gather.62.cloned.1.call-update) | async-done | bytes 1048592 | tf_op jit(solution)/shard_map/all_gather | solution.py:39
  782.9 22.3 %all-gather.58.cloned.1.call-done = bf16[512,1024]{1,0:T(8,128)(2,1)} async-done(((bf16[512,256]{1,0:T(8,128)(2,1)}), bf16[512,1024]{1,0:T(8,128)(2,1)}) %all-gather.58.cloned.1.call-update) | async-done | bytes 1048592 | tf_op jit(solution)/shard_map/all_gather | solution.py:39
  809.7 25.8 %all-gather.56.cloned.1.call-done = bf16[512,1024]{1,0:T(8,128)(2,1)} async-done(((bf16[512,256]{1,0:T(8,128)(2,1)}), bf16[512,1024]{1,0:T(8,128)(2,1)}) %all-gather.56.cloned.1.call-update) | async-done | bytes 1048592 | tf_op jit(solution)/shard_map/all_gather | solution.py:49
  863.9 28.7 %reduce-scatter.43.cloned.1.call-done = bf16[512,256]{1,0:T(8,128)(2,1)} async-done(((bf16[512,1024]{1,0:T(8,128)(2,1)}), bf16[512,256]{1,0:T(8,128)(2,1)}) %reduce-scatter.43.cloned.1.call-update) | async-done | bytes 262160 | tf_op jit(solution)/shard_map/reduce_scatter | solution.py:53
  907.1 28.3 %all-gather.60.cloned.1.call-done = bf16[512,1024]{1,0:T(8,128)(2,1)} async-done(((bf16[512,256]{1,0:T(8,128)(2,1)}), bf16[512,1024]{1,0:T(8,128)(2,1)}) %all-gather.60.cloned.1.call-update) | async-done | bytes 1048592 | tf_op jit(solution)/shard_map/all_gather | solution.py:49
  947.3 25.7 %reduce-scatter.45.cloned.1.call-done = bf16[512,256]{1,0:T(8,128)(2,1)} async-done(((bf16[512,1024]{1,0:T(8,128)(2,1)}), bf16[512,256]{1,0:T(8,128)(2,1)}) %reduce-scatter.45.cloned.1.call-update) | async-done | bytes 262160 | tf_op jit(solution)/shard_map/reduce_scatter | solution.py:53
  1001.1 20.1 %all-gather.42.cloned.1.call-done = bf16[512,1024]{1,0:T(8,128)(2,1)} async-done(((bf16[512,256]{1,0:T(8,128)(2,1)}), bf16[512,1024]{1,0:T(8,128)(2,1)}) %all-gather.42.cloned.1.call-update) | async-done | bytes 1048592 | tf_op jit(solution)/shard_map/all_gather | solution.py:39
  1056.1 25.2 %all-gather.64.cloned.1.call-done = bf16[512,1024]{1,0:T(8,128)(2,1)} async-done(((bf16[512,256]{1,0:T(8,128)(2,1)}), bf16[512,1024]{1,0:T(8,128)(2,1)}) %all-gather.64.cloned.1.call-update) | async-done | bytes 1048592 | tf_op jit(solution)/shard_map/all_gather | solution.py:49
  1088.8 20.9 %reduce-scatter.31.cloned.1.call-done = bf16[512,256]{1,0:T(8,128)(2,1)} async-done(((bf16[512,1024]{1,0:T(8,128)(2,1)}), bf16[512,256]{1,0:T(8,128)(2,1)}) %reduce-scatter.31.cloned.1.call-update) | async-done | bytes 262160 | tf_op jit(solution)/shard_map/reduce_scatter | solution.py:43
  1109.7 28.7 %reduce-scatter.49.cloned.1.call-done = bf16[512,256]{1,0:T(8,128)(2,1)} async-done(((bf16[512,1024]{1,0:T(8,128)(2,1)}), bf16[512,256]{1,0:T(8,128)(2,1)}) %reduce-scatter.49.cloned.1.call-update) | async-done | bytes 262160 | tf_op jit(solution)/shard_map/reduce_scatter | solution.py:53
  1151.4 28.8 %all-gather.68.cloned.1.call-done = bf16[512,1024]{1,0:T(8,128)(2,1)} async-done(((bf16[512,256]{1,0:T(8,128)(2,1)}), bf16[512,1024]{1,0:T(8,128)(2,1)}) %all-gather.68.cloned.1.call-update) | async-done | bytes 1048592 | tf_op jit(solution)/shard_map/all_gather | solution.py:49
  1257.0 24.2 %reduce-scatter.57.cloned.1.call-done = bf16[256,1024]{1,0:T(8,128)(2,1)} async-done(((bf16[1024,1024]{1,0:T(8,128)(2,1)}), bf16[256,1024]{1,0:T(8,128)(2,1)}) %reduce-scatter.57.cloned.1.call-update) | async-done | bytes 524304 | tf_op jit(solution)/shard_map/reduce_scatter | solution.py:339
  1283.3 29.8 %all-gather.44.cloned.1.call-done = bf16[512,1024]{1,0:T(8,128)(2,1)} async-done(((bf16[512,256]{1,0:T(8,128)(2,1)}), bf16[512,1024]{1,0:T(8,128)(2,1)}) %all-gather.44.cloned.1.call-update) | async-done | bytes 1048592 | tf_op jit(solution)/shard_map/all_gather | solution.py:39
  1319.2 30.4 %reduce-scatter.59.cloned.1.call-done = bf16[1024,256]{1,0:T(8,128)(2,1)} async-done(((bf16[1024,1024]{1,0:T(8,128)(2,1)}), bf16[1024,256]{1,0:T(8,128)(2,1)}) %reduce-scatter.59.cloned.1.call-update) | async-done | bytes 524304 | tf_op jit(solution)/shard_map/reduce_scatter | solution.py:345
  1351.7 25.7 %reduce-scatter.55.cloned.1.call-done = bf16[4,64,256]{2,1,0:T(8,128)(2,1)} async-done(((bf16[4,64,1024]{2,1,0:T(8,128)(2,1)}), bf16[4,64,256]{2,1,0:T(8,128)(2,1)}) %reduce-scatter.55.cloned.1.call-update) | async-done | bytes 131088 | tf_op jit(solution)/shard_map/reduce_scatter | solution.py:327
  1413.5 27.7 %reduce-scatter.33.cloned.1.call-done = bf16[512,256]{1,0:T(8,128)(2,1)} async-done(((bf16[512,1024]{1,0:T(8,128)(2,1)}), bf16[512,256]{1,0:T(8,128)(2,1)}) %reduce-scatter.33.cloned.1.call-update) | async-done | bytes 262160 | tf_op jit(solution)/shard_map/reduce_scatter | solution.py:43
  (513 shorter events, 572.1 us)
Async XLA Ops:
  41.5 94.4 %reduce-scatter.23.cloned.1.call-start = ((), (), s32[]{:S(2)}) async-start(), calls=%async_computation.21 | async-start | bytes 1310720 | tf_op jit(solution)/shard_map/reduce_scatter | solution.py:43
  109.1 99.0 %all-gather.72.cloned.1.call-start = ((), (), s32[]{:S(2)}) async-start(), calls=%async_computation.58 | async-start | bytes 2621440 | tf_op jit(solution)/shard_map/all_gather | solution.py:245
  109.7 130.4 %all-gather.36.cloned.1.call-start = ((), (), s32[]{:S(2)}) async-start(), calls=%async_computation.22 | async-start | bytes 1310720 | tf_op jit(solution)/shard_map/all_gather | solution.py:39
  148.3 123.6 %reduce-scatter.25.cloned.1.call-start = ((), (), s32[]{:S(2)}) async-start(), calls=%async_computation.23 | async-start | bytes 1310720 | tf_op jit(solution)/shard_map/reduce_scatter | solution.py:43
  246.2 68.7 %all-gather.46.cloned.1.call-start = ((), (), s32[]{:S(2)}) async-start(), calls=%async_computation.32 | async-start | bytes 1310720 | tf_op jit(solution)/shard_map/all_gather | solution.py:39
  286.2 63.2 %reduce-scatter.35.cloned.1.call-start = ((), (), s32[]{:S(2)}) async-start(), calls=%async_computation.33 | async-start | bytes 1310720 | tf_op jit(solution)/shard_map/reduce_scatter | solution.py:43
  323.6 66.1 %all-gather.38.cloned.1.call-start = ((), (), s32[]{:S(2)}) async-start(), calls=%async_computation.24 | async-start | bytes 1310720 | tf_op jit(solution)/shard_map/all_gather | solution.py:39
  362.9 87.5 %all-gather.48.cloned.1.call-start = ((), (), s32[]{:S(2)}) async-start(), calls=%async_computation.34 | async-start | bytes 1310720 | tf_op jit(solution)/shard_map/all_gather | solution.py:49
  364.3 114.6 %reduce-scatter.27.cloned.1.call-start = ((), (), s32[]{:S(2)}) async-start(), calls=%async_computation.25 | async-start | bytes 1310720 | tf_op jit(solution)/shard_map/reduce_scatter | solution.py:43
  402.9 104.5 %reduce-scatter.37.cloned.1.call-start = ((), (), s32[]{:S(2)}) async-start(), calls=%async_computation.36 | async-start | bytes 1310720 | tf_op jit(solution)/shard_map/reduce_scatter | solution.py:53
  459.4 90.1 %all-gather.40.cloned.1.call-start = ((), (), s32[]{:S(2)}) async-start(), calls=%async_computation.26 | async-start | bytes 1310720 | tf_op jit(solution)/shard_map/all_gather | solution.py:39
  555.7 69.9 %all-gather.52.cloned.1.call-start = ((), (), s32[]{:S(2)}) async-start(), calls=%async_computation.37 | async-start | bytes 1310720 | tf_op jit(solution)/shard_map/all_gather | solution.py:49
  596.8 66.3 %reduce-scatter.39.cloned.1.call-start = ((), (), s32[]{:S(2)}) async-start(), calls=%async_computation.38 | async-start | bytes 1310720 | tf_op jit(solution)/shard_map/reduce_scatter | solution.py:53
  702.4 72.4 %all-gather.62.cloned.1.call-start = ((), (), s32[]{:S(2)}) async-start(), calls=%async_computation.46 | async-start | bytes 1310720 | tf_op jit(solution)/shard_map/all_gather | solution.py:39
  748.5 87.0 %all-gather.56.cloned.1.call-start = ((), (), s32[]{:S(2)}) async-start(), calls=%async_computation.41 | async-start | bytes 1310720 | tf_op jit(solution)/shard_map/all_gather | solution.py:49
  754.6 109.3 %reduce-scatter.47.cloned.1.call-start = ((), (), s32[]{:S(2)}) async-start(), calls=%async_computation.47 | async-start | bytes 1310720 | tf_op jit(solution)/shard_map/reduce_scatter | solution.py:43
  782.9 109.7 %reduce-scatter.43.cloned.1.call-start = ((), (), s32[]{:S(2)}) async-start(), calls=%async_computation.43 | async-start | bytes 1310720 | tf_op jit(solution)/shard_map/reduce_scatter | solution.py:53
  844.7 90.8 %all-gather.60.cloned.1.call-start = ((), (), s32[]{:S(2)}) async-start(), calls=%async_computation.44 | async-start | bytes 1310720 | tf_op jit(solution)/shard_map/all_gather | solution.py:49
  906.6 66.4 %reduce-scatter.45.cloned.1.call-start = ((), (), s32[]{:S(2)}) async-start(), calls=%async_computation.45 | async-start | bytes 1310720 | tf_op jit(solution)/shard_map/reduce_scatter | solution.py:53
  947.2 74.0 %all-gather.42.cloned.1.call-start = ((), (), s32[]{:S(2)}) async-start(), calls=%async_computation.28 | async-start | bytes 1310720 | tf_op jit(solution)/shard_map/all_gather | solution.py:39
  994.6 86.6 %all-gather.64.cloned.1.call-start = ((), (), s32[]{:S(2)}) async-start(), calls=%async_computation.48 | async-start | bytes 1310720 | tf_op jit(solution)/shard_map/all_gather | solution.py:49
  1000.8 108.9 %reduce-scatter.31.cloned.1.call-start = ((), (), s32[]{:S(2)}) async-start(), calls=%async_computation.29 | async-start | bytes 1310720 | tf_op jit(solution)/shard_map/reduce_scatter | solution.py:43
  1034.3 104.1 %reduce-scatter.49.cloned.1.call-start = ((), (), s32[]{:S(2)}) async-start(), calls=%async_computation.50 | async-start | bytes 1310720 | tf_op jit(solution)/shard_map/reduce_scatter | solution.py:53
  1088.7 91.4 %all-gather.68.cloned.1.call-start = ((), (), s32[]{:S(2)}) async-start(), calls=%async_computation.51 | async-start | bytes 1310720 | tf_op jit(solution)/shard_map/all_gather | solution.py:49
  1151.4 66.4 %reduce-scatter.51.cloned.1.call-start = ((), (), s32[]{:S(2)}) async-start(), calls=%async_computation.52 | async-start | bytes 1310720 | tf_op jit(solution)/shard_map/reduce_scatter | solution.py:53
  1192.0 63.6 %reduce-scatter.61.cloned.1.call-start = ((), (), s32[]{:S(2)}) async-start(), calls=%async_computation.60 | async-start | bytes 40960
  1199.8 81.4 %reduce-scatter.57.cloned.1.call-start = ((), (), s32[]{:S(2)}) async-start(), calls=%async_computation.55 | async-start | bytes 2621440 | tf_op jit(solution)/shard_map/reduce_scatter | solution.py:339
  1205.0 108.1 %all-gather.44.cloned.1.call-start = ((), (), s32[]{:S(2)}) async-start(), calls=%async_computation.30 | async-start | bytes 1310720 | tf_op jit(solution)/shard_map/all_gather | solution.py:39
  1229.5 120.1 %reduce-scatter.59.cloned.1.call-start = ((), (), s32[]{:S(2)}) async-start(), calls=%async_computation.56 | async-start | bytes 2621440 | tf_op jit(solution)/shard_map/reduce_scatter | solution.py:345
  1238.4 139.1 %reduce-scatter.55.cloned.1.call-start = ((), (), s32[]{:S(2)}) async-start(), calls=%async_computation.54 | async-start | bytes 655360 | tf_op jit(solution)/shard_map/reduce_scatter | solution.py:327
  1245.5 166.0 %reduce-scatter.53.cloned.1.call-start = ((), (), s32[]{:S(2)}) async-start(), calls=%async_computation.53 | async-start | bytes 1966080 | tf_op jit(solution)/shard_map/reduce_scatter | solution.py:321
  1252.1 189.0 %reduce-scatter.33.cloned.1.call-start = ((), (), s32[]{:S(2)}) async-start(), calls=%async_computation.31 | async-start | bytes 1310720 | tf_op jit(solution)/shard_map/reduce_scatter | solution.py:43
  (116 other events, 3701.3 us)
Sparse Core Ops, SparseCore 0:
  40.9 26.1 all-gather.33
  68.9 28.9 all-gather.69
  108.6 27.2 reduce-scatter.22
  137.6 33.5 all-gather.73
  172.9 35.1 all-gather.71
  210.1 29.9 all-gather.35
  246.3 25.5 reduce-scatter.24
  286.3 28.5 all-gather.45
  323.8 25.5 reduce-scatter.34
  361.0 28.6 all-gather.37
  391.9 28.2 all-gather.49
  422.1 28.2 all-gather.47
  481.6 25.7 reduce-scatter.36
  520.9 28.6 all-gather.39
  555.8 25.5 reduce-scatter.28
  596.9 28.5 all-gather.51
  665.8 28.4 all-gather.53
  746.7 28.0 all-gather.61
  776.9 28.2 all-gather.57
  807.3 28.2 all-gather.55
  866.8 25.7 reduce-scatter.42
  906.7 28.6 all-gather.59
  993.1 28.0 all-gather.41
  1023.3 28.2 all-gather.65
  1053.0 28.2 all-gather.63
  1112.6 25.7 reduce-scatter.48
  1151.5 28.6 all-gather.67
  1245.9 35.1 reduce-scatter.56
  1283.1 29.9 all-gather.43
  1316.1 33.4 reduce-scatter.58
  1380.4 31.0 reduce-scatter.52
  1413.8 27.2 reduce-scatter.32
  (9 shorter events, 226.2 us)
where the time goes:
time: 1460 us; the launch traced here: 1450 us
  waiting for transfers between devices  991 us (68%)
  blocking collectives  168 us (12%)
  matrix products  166 us (11%)
  other arithmetic  73.8 us (5%)
  local copies, waits for them, and re-layouts  24.1 us (2%)
  between operations  18.7 us (1%)
    all_gather x12, waiting for transfers between devices, full_rows(): return lax.all_gather(piece, 'tensor', axis=1, tiled=True)  273 us
    reduce_scatter x9, waiting for transfers between devices, head_sums(): lax.psum_scatter(partial_rows.astype(jnp.bfloat16), 'tensor', scatter_dim...  216 us
    all_gather x6, waiting for transfers between devices, grad_full(): return lax.all_gather(piece, 'tensor', axis=1, tiled=True)  162 us
    reduce_scatter x6, waiting for transfers between devices, back_sums(): lax.psum_scatter(partial_rows.astype(jnp.bfloat16), 'tensor', scatter_dim...  150 us
    psum x11, blocking collectives, row_totals(): return lax.psum((jnp.sum(first, axis=1), jnp.sum(second, axis=1)), 'tensor')  120 us
    all_gather x1, waiting for transfers between devices, body(): lax.all_gather(up_weight[0], 'seq', axis=0, tiled=True)  36.9 us
    all_gather x1, waiting for transfers between devices, body(): lax.all_gather(qkv_weight[0], 'seq', axis=0, tiled=True)  30.9 us
    reduce_scatter x1, waiting for transfers between devices, body(): lax.psum_scatter(totals[10].astype(jnp.bfloat16), 'seq', scatter_dimensio...  30.4 us
  transfers between devices with their start and end apart: 45, of which 44 were waited for; matrix products, arithmetic and copies ran while one was open for 10% of the time, Pallas kernels for 0%

commit v1 on v0

--- a/solution.py
+++ b/solution.py
@@ -8,6 +8,27 @@
 MB = 2
 epsilon = 1e-05
 floor_value = -1e30
+
+
+def ring_gather(array, axis, dim):
+    length, mine, rows = (lax.axis_size(axis), lax.axis_index(axis), array.shape[dim])
+    right = [(i, (i + 1) % length) for i in range(length)]
+    left = [(i, (i - 1) % length) for i in range(length)]
+    whole = jnp.zeros((*array.shape[:dim], length * rows, *array.shape[dim + 1 :]), array.dtype)
+    whole = lax.dynamic_update_slice_in_dim(whole, array, mine * rows, axis=dim)
+    from_left = from_right = array
+    middle = length // 2
+    for turn in range(1, middle + 1):
+        from_left = lax.ppermute(from_left, axis, right)
+        whole = lax.dynamic_update_slice_in_dim(
+            whole, from_left, (mine - turn) % length * rows, axis=dim
+        )
+        if turn < length - middle:
+            from_right = lax.ppermute(from_right, axis, left)
+            whole = lax.dynamic_update_slice_in_dim(
+                whole, from_right, (mine + turn) % length * rows, axis=dim
+            )
+    return whole
 
 
 def passed_along(shard, axis, by):
@@ -46,7 +67,7 @@
 
 
 def grad_full(piece):
-    return lax.all_gather(piece, "tensor", axis=1, tiled=True)
+    return ring_gather(piece, "tensor", 1)
 
 
 def back_sums(partial_rows):

time: 1460 us -> 1370 us (0.938)
  waiting for transfers between devices: 991 us -> 882 us
  starting transfers between devices: 9.04 us -> 29.9 us
  local copies, waits for them, and re-layouts: 24.1 us -> 38.8 us
    all_gather x6 -> x0, waiting for transfers between devices: 162 us -> none  [grad_full(): return lax.all_gather(piece, 'tensor', axis=1, tiled=True)]
    ppermute x0 -> x18, waiting for transfers between devices: none -> 111 us  [the longest x12 81 us: ring_gather(): from_left = lax.ppermute(from_left, axis, right)]
    all_gather x12, waiting for transfers between devices: 273 us -> 226 us  [full_rows(): return lax.all_gather(piece, 'tensor', axis=1, tiled=True)]
    ppermute x0 -> x18, starting transfers between devices: none -> 22.5 us  [the longest x6 14.1 us: ring_gather(): from_right = lax.ppermute(from_right, axis, left)]
    reduce_scatter x1, waiting for transfers between devices: 25.7 us -> 10.1 us  [body(): lax.psum_scatter(totals[4].astype(jnp.bfloat16), 'seq', scatter_dimension...]
  transfers between devices with their start and end apart: 45 -> 57, of which waited for: 44 -> 53; matrix products, arithmetic and copies ran while one was open for 10% -> 11% of each run, Pallas kernels for 0% -> 0%
where the time goes in v1:
time: 1370 us; the launch traced here: 1360 us
  waiting for transfers between devices  882 us (64%)
  blocking collectives  169 us (12%)
  matrix products  153 us (11%)
  other arithmetic  71.9 us (5%)
  local copies, waits for them, and re-layouts  38.8 us (3%)
  starting transfers between devices  29.9 us (2%)
  between operations  18.3 us (1%)
    all_gather x12, waiting for transfers between devices, full_rows(): return lax.all_gather(piece, 'tensor', axis=1, tiled=True)  226 us
    reduce_scatter x9, waiting for transfers between devices, head_sums(): lax.psum_scatter(partial_rows.astype(jnp.bfloat16), 'tensor', scatter_dim...  217 us
    reduce_scatter x6, waiting for transfers between devices, back_sums(): lax.psum_scatter(partial_rows.astype(jnp.bfloat16), 'tensor', scatter_dim...  143 us
    psum x11, blocking collectives, row_totals(): return lax.psum((jnp.sum(first, axis=1), jnp.sum(second, axis=1)), 'tensor')  121 us
    ppermute x12, waiting for transfers between devices, ring_gather(): from_left = lax.ppermute(from_left, axis, right)  81 us
    all_gather x1, waiting for transfers between devices, body(): lax.all_gather(up_weight[0], 'seq', axis=0, tiled=True)  36.9 us
    reduce_scatter x1, waiting for transfers between devices, body(): lax.psum_scatter(totals[10].astype(jnp.bfloat16), 'seq', scatter_dimensio...  35.9 us
    all_gather x1, waiting for transfers between devices, body(): lax.all_gather(qkv_weight[0], 'seq', axis=0, tiled=True)  30.9 us
  transfers between devices with their start and end apart: 57, of which 53 were waited for; matrix products, arithmetic and copies ran while one was open for 11% of the time, Pallas kernels for 0%

profile of v1, /device:TPU:0, one launch (start us, length us, event | category | flops | bytes accessed | tf_op | source)
XLA Modules:
  0.0 1362.1 jit_solution(904458426868130272)
XLA Ops:
  49.9 12.1 all-gather.4
  67.1 30.9 %all-gather.52.cloned.1.call-done = bf16[1,1024,4,192]{1,3,2,0:T(8,128)(2,1)} async-done(((bf16[1,256,4,192]{1,3,2,0:T(8,128)(2,1)}), bf16[1,1024,4,192]{1,3,2,0:T(8,128)(2,1)}) %all-gather.52.cloned.1.call-update) | async-done | bytes 1572880 | tf_op jit(solution)/shard_map/all_gather | solution.py:260
  109.7 26.2 %reduce-scatter.23.cloned.1.call-done = bf16[512,256]{1,0:T(8,128)(2,1)} async-done(((bf16[512,1024]{1,0:T(8,128)(2,1)}), bf16[512,256]{1,0:T(8,128)(2,1)}) %reduce-scatter.23.cloned.1.call-update) | async-done | bytes 262160 | tf_op jit(solution)/shard_map/reduce_scatter | solution.py:64
  156.5 14.8 %all-gather.56.cloned.1.call-done = bf16[1,1024,1024]{2,1,0:T(8,128)(2,1)} async-done(((bf16[1,1024,256]{2,1,0:T(8,128)(2,1)}), bf16[1,1024,1024]{2,1,0:T(8,128)(2,1)}) %all-gather.56.cloned.1.call-update) | async-done | bytes 2097168 | tf_op jit(solution)/shard_map/all_gather | solution.py:268
  171.2 36.9 %all-gather.54.cloned.1.call-done = bf16[1,1024,1024]{2,1,0:T(8,128)(2,1)} async-done(((bf16[1,256,1024]{2,1,0:T(8,128)(2,1)}), bf16[1,1024,1024]{2,1,0:T(8,128)(2,1)}) %all-gather.54.cloned.1.call-update) | async-done | bytes 2097168 | tf_op jit(solution)/shard_map/all_gather | solution.py:266
  208.1 31.9 %all-gather.30.cloned.1.call-done = bf16[512,1024]{1,0:T(8,128)(2,1)} async-done(((bf16[512,256]{1,0:T(8,128)(2,1)}), bf16[512,1024]{1,0:T(8,128)(2,1)}) %all-gather.30.cloned.1.call-update) | async-done | bytes 1048592 | tf_op jit(solution)/shard_map/all_gather | solution.py:60
  246.3 25.7 %reduce-scatter.25.cloned.1.call-done = bf16[512,256]{1,0:T(8,128)(2,1)} async-done(((bf16[512,1024]{1,0:T(8,128)(2,1)}), bf16[512,256]{1,0:T(8,128)(2,1)}) %reduce-scatter.25.cloned.1.call-update) | async-done | bytes 262160 | tf_op jit(solution)/shard_map/reduce_scatter | solution.py:64
  286.7 28.2 %all-gather.40.cloned.1.call-done = bf16[512,1024]{1,0:T(8,128)(2,1)} async-done(((bf16[512,256]{1,0:T(8,128)(2,1)}), bf16[512,1024]{1,0:T(8,128)(2,1)}) %all-gather.40.cloned.1.call-update) | async-done | bytes 1048592 | tf_op jit(solution)/shard_map/all_gather | solution.py:60
  323.9 25.5 %reduce-scatter.35.cloned.1.call-done = bf16[512,256]{1,0:T(8,128)(2,1)} async-done(((bf16[512,1024]{1,0:T(8,128)(2,1)}), bf16[512,256]{1,0:T(8,128)(2,1)}) %reduce-scatter.35.cloned.1.call-update) | async-done | bytes 262160 | tf_op jit(solution)/shard_map/reduce_scatter | solution.py:64
  364.8 25.0 %all-gather.32.cloned.1.call-done = bf16[512,1024]{1,0:T(8,128)(2,1)} async-done(((bf16[512,256]{1,0:T(8,128)(2,1)}), bf16[512,1024]{1,0:T(8,128)(2,1)}) %all-gather.32.cloned.1.call-update) | async-done | bytes 1048592 | tf_op jit(solution)/shard_map/all_gather | solution.py:60
  442.4 16.4 %reduce-scatter.27.cloned.1.call-done = bf16[512,256]{1,0:T(8,128)(2,1)} async-done(((bf16[512,1024]{1,0:T(8,128)(2,1)}), bf16[512,256]{1,0:T(8,128)(2,1)}) %reduce-scatter.27.cloned.1.call-update) | async-done | bytes 262160 | tf_op jit(solution)/shard_map/reduce_scatter | solution.py:64
  458.8 28.1 %reduce-scatter.37.cloned.1.call-done = bf16[512,256]{1,0:T(8,128)(2,1)} async-done(((bf16[512,1024]{1,0:T(8,128)(2,1)}), bf16[512,256]{1,0:T(8,128)(2,1)}) %reduce-scatter.37.cloned.1.call-update) | async-done | bytes 262160 | tf_op jit(solution)/shard_map/reduce_scatter | solution.py:74
  500.3 28.8 %all-gather.34.cloned.1.call-done = bf16[512,1024]{1,0:T(8,128)(2,1)} async-done(((bf16[512,256]{1,0:T(8,128)(2,1)}), bf16[512,1024]{1,0:T(8,128)(2,1)}) %all-gather.34.cloned.1.call-update) | async-done | bytes 1048592 | tf_op jit(solution)/shard_map/all_gather | solution.py:60
  535.2 25.7 %reduce-scatter.29.cloned.1.call-done = bf16[512,256]{1,0:T(8,128)(2,1)} async-done(((bf16[512,1024]{1,0:T(8,128)(2,1)}), bf16[512,256]{1,0:T(8,128)(2,1)}) %reduce-scatter.29.cloned.1.call-update) | async-done | bytes 262160 | tf_op jit(solution)/shard_map/reduce_scatter | solution.py:64
  604.2 25.4 %reduce-scatter.39.cloned.1.call-done = bf16[512,256]{1,0:T(8,128)(2,1)} async-done(((bf16[512,1024]{1,0:T(8,128)(2,1)}), bf16[512,256]{1,0:T(8,128)(2,1)}) %reduce-scatter.39.cloned.1.call-update) | async-done | bytes 262160 | tf_op jit(solution)/shard_map/reduce_scatter | solution.py:74
  632.5 28.3 %all-gather.44.cloned.1.call-done = bf16[512,1024]{1,0:T(8,128)(2,1)} async-done(((bf16[512,256]{1,0:T(8,128)(2,1)}), bf16[512,1024]{1,0:T(8,128)(2,1)}) %all-gather.44.cloned.1.call-update) | async-done | bytes 1048592 | tf_op jit(solution)/shard_map/all_gather | solution.py:60
  669.6 25.7 %reduce-scatter.41.cloned.1.call-done = bf16[512,256]{1,0:T(8,128)(2,1)} async-done(((bf16[512,1024]{1,0:T(8,128)(2,1)}), bf16[512,256]{1,0:T(8,128)(2,1)}) %reduce-scatter.41.cloned.1.call-update) | async-done | bytes 262160 | tf_op jit(solution)/shard_map/reduce_scatter | solution.py:64
  696.5 16.8 %all-reduce.17 = (f32[512]{0:T(512)S(1)}, f32[512]{0:T(512)S(1)}, f32[512]{0:T(512)S(1)}, f32[512]{0:T(512)S(1)}, f32[512]{0:T(512)S(1)}, /*index=5*/f32[512]{0:T(512)}) all-reduce(f32[512]{0:T(512)S(1)} %get-tuple-element.31, f32[512]{0:T(512)S(1)} %get-tuple-element.30, ...), channel_id=1, replica_groups=mesh['section'=2,'seq'=4,'tensor'=4] {'tensor'}, use_global_device_ids=true, to_apply=%region_66.67 | all-reduce | flops 3072 | bytes 24576 | tf_op jit(solution)/shard_map/psum | solution.py:41
  772.0 17.5 %all-gather.48.cloned.1.call-done = bf16[512,1024]{1,0:T(8,128)(2,1)} async-done(((bf16[512,256]{1,0:T(8,128)(2,1)}), bf16[512,1024]{1,0:T(8,128)(2,1)}) %all-gather.48.cloned.1.call-update) | async-done | bytes 1048592 | tf_op jit(solution)/shard_map/all_gather | solution.py:60
  797.5 19.9 %reduce-scatter.43.cloned.1.call-done = bf16[512,256]{1,0:T(8,128)(2,1)} async-done(((bf16[512,1024]{1,0:T(8,128)(2,1)}), bf16[512,256]{1,0:T(8,128)(2,1)}) %reduce-scatter.43.cloned.1.call-update) | async-done | bytes 262160 | tf_op jit(solution)/shard_map/reduce_scatter | solution.py:74
  817.4 28.1 %reduce-scatter.47.cloned.1.call-done = bf16[512,256]{1,0:T(8,128)(2,1)} async-done(((bf16[512,1024]{1,0:T(8,128)(2,1)}), bf16[512,256]{1,0:T(8,128)(2,1)}) %reduce-scatter.47.cloned.1.call-update) | async-done | bytes 262160 | tf_op jit(solution)/shard_map/reduce_scatter | solution.py:64
  887.5 25.5 %reduce-scatter.45.cloned.1.call-done = bf16[512,256]{1,0:T(8,128)(2,1)} async-done(((bf16[512,1024]{1,0:T(8,128)(2,1)}), bf16[512,256]{1,0:T(8,128)(2,1)}) %reduce-scatter.45.cloned.1.call-update) | async-done | bytes 262160 | tf_op jit(solution)/shard_map/reduce_scatter | solution.py:74
  914.9 16.8 %all-reduce.15 = (f32[512]{0:T(512)}, f32[512]{0:T(512)}, f32[512]{0:T(512)S(1)}, f32[512]{0:T(512)S(1)}, f32[512]{0:T(512)}, /*index=5*/f32[512]{0:T(512)S(1)}) all-reduce(f32[512]{0:T(512)S(1)} %get-tuple-element.147, f32[512]{0:T(512)S(1)} %get-tuple-element.148, ...), channel_id=1, replica_groups=mesh['section'=2,'seq'=4,'tensor'=4] {'tensor'}, use_global_device_ids=true, to_apply=%region_27.28 | all-reduce | flops 3072 | bytes 24576 | tf_op jit(solution)/shard_map/psum | solution.py:41
  941.6 24.9 %all-gather.36.cloned.1.call-done = bf16[512,1024]{1,0:T(8,128)(2,1)} async-done(((bf16[512,256]{1,0:T(8,128)(2,1)}), bf16[512,1024]{1,0:T(8,128)(2,1)}) %all-gather.36.cloned.1.call-update) | async-done | bytes 1048592 | tf_op jit(solution)/shard_map/all_gather | solution.py:60
  1019.1 16.4 %reduce-scatter.31.cloned.1.call-done = bf16[512,256]{1,0:T(8,128)(2,1)} async-done(((bf16[512,1024]{1,0:T(8,128)(2,1)}), bf16[512,256]{1,0:T(8,128)(2,1)}) %reduce-scatter.31.cloned.1.call-update) | async-done | bytes 262160 | tf_op jit(solution)/shard_map/reduce_scatter | solution.py:64
  1035.5 28.0 %reduce-scatter.49.cloned.1.call-done = bf16[512,256]{1,0:T(8,128)(2,1)} async-done(((bf16[512,1024]{1,0:T(8,128)(2,1)}), bf16[512,256]{1,0:T(8,128)(2,1)}) %reduce-scatter.49.cloned.1.call-update) | async-done | bytes 262160 | tf_op jit(solution)/shard_map/reduce_scatter | solution.py:74
  1112.9 16.1 %reduce-scatter.51.cloned.1.call-done = bf16[512,256]{1,0:T(8,128)(2,1)} async-done(((bf16[512,1024]{1,0:T(8,128)(2,1)}), bf16[512,256]{1,0:T(8,128)(2,1)}) %reduce-scatter.51.cloned.1.call-update) | async-done | bytes 262160 | tf_op jit(solution)/shard_map/reduce_scatter | solution.py:74
  1184.4 30.5 %all-gather.38.cloned.1.call-done = bf16[512,1024]{1,0:T(8,128)(2,1)} async-done(((bf16[512,256]{1,0:T(8,128)(2,1)}), bf16[512,1024]{1,0:T(8,128)(2,1)}) %all-gather.38.cloned.1.call-update) | async-done | bytes 1048592 | tf_op jit(solution)/shard_map/all_gather | solution.py:60
  1221.0 30.4 %reduce-scatter.57.cloned.1.call-done = bf16[256,1024]{1,0:T(8,128)(2,1)} async-done(((bf16[1024,1024]{1,0:T(8,128)(2,1)}), bf16[256,1024]{1,0:T(8,128)(2,1)}) %reduce-scatter.57.cloned.1.call-update) | async-done | bytes 524304 | tf_op jit(solution)/shard_map/reduce_scatter | solution.py:360
  1253.5 35.9 %reduce-scatter.59.cloned.1.call-done = bf16[1024,256]{1,0:T(8,128)(2,1)} async-done(((bf16[1024,1024]{1,0:T(8,128)(2,1)}), bf16[1024,256]{1,0:T(8,128)(2,1)}) %reduce-scatter.59.cloned.1.call-update) | async-done | bytes 524304 | tf_op jit(solution)/shard_map/reduce_scatter | solution.py:366
  1306.2 17.3 %reduce-scatter.53.cloned.1.call-done = bf16[256,4,192]{0,2,1:T(8,128)(2,1)} async-done(((bf16[1024,4,192]{0,2,1:T(8,128)(2,1)}), bf16[256,4,192]{0,2,1:T(8,128)(2,1)}) %reduce-scatter.53.cloned.1.call-update) | async-done | bytes 393232 | tf_op jit(solution)/shard_map/reduce_scatter | solution.py:342
  1325.5 27.7 %reduce-scatter.33.cloned.1.call-done = bf16[512,256]{1,0:T(8,128)(2,1)} async-done(((bf16[512,1024]{1,0:T(8,128)(2,1)}), bf16[512,256]{1,0:T(8,128)(2,1)}) %reduce-scatter.33.cloned.1.call-update) | async-done | bytes 262160 | tf_op jit(solution)/shard_map/reduce_scatter | solution.py:64
  (545 shorter events, 556.5 us)
Async XLA Ops:
  41.5 94.4 %reduce-scatter.23.cloned.1.call-start = ((), (), s32[]{:S(2)}) async-start(), calls=%async_computation.21 | async-start | bytes 1310720 | tf_op jit(solution)/shard_map/reduce_scatter | solution.py:64
  108.5 62.7 %all-gather.56.cloned.1.call-start = ((), (), s32[]{:S(2)}) async-start(), calls=%async_computation.53 | async-start | bytes 2621440 | tf_op jit(solution)/shard_map/all_gather | solution.py:268
  109.1 99.1 %all-gather.54.cloned.1.call-start = ((), (), s32[]{:S(2)}) async-start(), calls=%async_computation.52 | async-start | bytes 2621440 | tf_op jit(solution)/shard_map/all_gather | solution.py:266
  109.7 130.4 %all-gather.30.cloned.1.call-start = ((), (), s32[]{:S(2)}) async-start(), calls=%async_computation.22 | async-start | bytes 1310720 | tf_op jit(solution)/shard_map/all_gather | solution.py:60
  148.3 123.6 %reduce-scatter.25.cloned.1.call-start = ((), (), s32[]{:S(2)}) async-start(), calls=%async_computation.23 | async-start | bytes 1310720 | tf_op jit(solution)/shard_map/reduce_scatter | solution.py:64
  246.2 68.7 %all-gather.40.cloned.1.call-start = ((), (), s32[]{:S(2)}) async-start(), calls=%async_computation.32 | async-start | bytes 1310720 | tf_op jit(solution)/shard_map/all_gather | solution.py:60
  286.2 63.1 %reduce-scatter.35.cloned.1.call-start = ((), (), s32[]{:S(2)}) async-start(), calls=%async_computation.33 | async-start | bytes 1310720 | tf_op jit(solution)/shard_map/reduce_scatter | solution.py:64
  323.6 66.1 %all-gather.32.cloned.1.call-start = ((), (), s32[]{:S(2)}) async-start(), calls=%async_computation.24 | async-start | bytes 1310720 | tf_op jit(solution)/shard_map/all_gather | solution.py:60
  360.9 69.7 %all-gather.42.cloned.1.call-start = ((), (), s32[]{:S(2)}) async-start(), calls=%async_computation.34 | async-start | bytes 1310720 | tf_op jit(solution)/shard_map/all_gather | solution.py:60
  364.5 94.3 %reduce-scatter.27.cloned.1.call-start = ((), (), s32[]{:S(2)}) async-start(), calls=%async_computation.25 | async-start | bytes 1310720 | tf_op jit(solution)/shard_map/reduce_scatter | solution.py:64
  402.9 84.0 %reduce-scatter.37.cloned.1.call-start = ((), (), s32[]{:S(2)}) async-start(), calls=%async_computation.35 | async-start | bytes 1310720 | tf_op jit(solution)/shard_map/reduce_scatter | solution.py:74
  442.3 86.7 %all-gather.34.cloned.1.call-start = ((), (), s32[]{:S(2)}) async-start(), calls=%async_computation.26 | async-start | bytes 1310720 | tf_op jit(solution)/shard_map/all_gather | solution.py:60
  500.2 60.6 %reduce-scatter.29.cloned.1.call-start = ((), (), s32[]{:S(2)}) async-start(), calls=%async_computation.27 | async-start | bytes 1310720 | tf_op jit(solution)/shard_map/reduce_scatter | solution.py:64
  535.1 94.5 %reduce-scatter.39.cloned.1.call-start = ((), (), s32[]{:S(2)}) async-start(), calls=%async_computation.36 | async-start | bytes 1310720 | tf_op jit(solution)/shard_map/reduce_scatter | solution.py:74
  632.3 63.0 %reduce-scatter.41.cloned.1.call-start = ((), (), s32[]{:S(2)}) async-start(), calls=%async_computation.38 | async-start | bytes 1310720 | tf_op jit(solution)/shard_map/reduce_scatter | solution.py:64
  669.6 90.5 %all-gather.46.cloned.1.call-start = ((), (), s32[]{:S(2)}) async-start(), calls=%async_computation.39 | async-start | bytes 1310720 | tf_op jit(solution)/shard_map/all_gather | solution.py:60
  715.2 74.3 %all-gather.48.cloned.1.call-start = ((), (), s32[]{:S(2)}) async-start(), calls=%async_computation.42 | async-start | bytes 1310720 | tf_op jit(solution)/shard_map/all_gather | solution.py:60
  726.5 90.9 %reduce-scatter.43.cloned.1.call-start = ((), (), s32[]{:S(2)}) async-start(), calls=%async_computation.40 | async-start | bytes 1310720 | tf_op jit(solution)/shard_map/reduce_scatter | solution.py:74
  771.8 73.8 %reduce-scatter.47.cloned.1.call-start = ((), (), s32[]{:S(2)}) async-start(), calls=%async_computation.43 | async-start | bytes 1310720 | tf_op jit(solution)/shard_map/reduce_scatter | solution.py:64
  797.5 115.5 %reduce-scatter.45.cloned.1.call-start = ((), (), s32[]{:S(2)}) async-start(), calls=%async_computation.41 | async-start | bytes 1310720 | tf_op jit(solution)/shard_map/reduce_scatter | solution.py:74
  887.5 79.0 %all-gather.36.cloned.1.call-start = ((), (), s32[]{:S(2)}) async-start(), calls=%async_computation.28 | async-start | bytes 1310720 | tf_op jit(solution)/shard_map/all_gather | solution.py:60
  933.4 74.4 %all-gather.50.cloned.1.call-start = ((), (), s32[]{:S(2)}) async-start(), calls=%async_computation.44 | async-start | bytes 1310720 | tf_op jit(solution)/shard_map/all_gather | solution.py:60
  939.1 96.4 %reduce-scatter.31.cloned.1.call-start = ((), (), s32[]{:S(2)}) async-start(), calls=%async_computation.29 | async-start | bytes 1310720 | tf_op jit(solution)/shard_map/reduce_scatter | solution.py:64
  979.7 83.8 %reduce-scatter.49.cloned.1.call-start = ((), (), s32[]{:S(2)}) async-start(), calls=%async_computation.45 | async-start | bytes 1310720 | tf_op jit(solution)/shard_map/reduce_scatter | solution.py:74
  1019.0 110.0 %reduce-scatter.51.cloned.1.call-start = ((), (), s32[]{:S(2)}) async-start(), calls=%async_computation.46 | async-start | bytes 1310720 | tf_op jit(solution)/shard_map/reduce_scatter | solution.py:74
  1103.4 67.8 %reduce-scatter.61.cloned.1.call-start = ((), (), s32[]{:S(2)}) async-start(), calls=%async_computation.54 | async-start | bytes 40960
  1109.5 73.3 %reduce-scatter.55.cloned.1.call-start = ((), (), s32[]{:S(2)}) async-start(), calls=%async_computation.48 | async-start | bytes 655360 | tf_op jit(solution)/shard_map/reduce_scatter | solution.py:348
  1112.7 102.2 %all-gather.38.cloned.1.call-start = ((), (), s32[]{:S(2)}) async-start(), calls=%async_computation.30 | async-start | bytes 1310720 | tf_op jit(solution)/shard_map/all_gather | solution.py:60
  1141.3 110.1 %reduce-scatter.57.cloned.1.call-start = ((), (), s32[]{:S(2)}) async-start(), calls=%async_computation.49 | async-start | bytes 2621440 | tf_op jit(solution)/shard_map/reduce_scatter | solution.py:360
  1148.9 140.6 %reduce-scatter.59.cloned.1.call-start = ((), (), s32[]{:S(2)}) async-start(), calls=%async_computation.50 | async-start | bytes 2621440 | tf_op jit(solution)/shard_map/reduce_scatter | solution.py:366
  1160.4 163.2 %reduce-scatter.53.cloned.1.call-start = ((), (), s32[]{:S(2)}) async-start(), calls=%async_computation.47 | async-start | bytes 1966080 | tf_op jit(solution)/shard_map/reduce_scatter | solution.py:342
  1168.9 184.3 %reduce-scatter.33.cloned.1.call-start = ((), (), s32[]{:S(2)}) async-start(), calls=%async_computation.31 | async-start | bytes 1310720 | tf_op jit(solution)/shard_map/reduce_scatter | solution.py:64
  (120 other events, 2620.2 us)
Sparse Core Ops, SparseCore 0:
  40.9 26.1 all-gather.27
  68.9 28.9 all-gather.51
  108.6 27.2 reduce-scatter.22
  137.6 33.5 all-gather.55
  172.9 35.1 all-gather.53
  210.1 29.9 all-gather.29
  246.3 25.5 reduce-scatter.24
  286.3 28.5 all-gather.39
  323.7 25.5 reduce-scatter.34
  361.0 28.6 all-gather.31
  391.9 38.6 all-gather.41
  433.3 25.4 reduce-scatter.26
  461.1 25.7 reduce-scatter.36
  500.3 28.6 all-gather.33
  535.2 25.5 reduce-scatter.28
  632.4 28.4 all-gather.43
  669.7 25.5 reduce-scatter.40
  715.4 43.2 all-gather.45
  760.6 28.8 all-gather.47
  791.8 25.5 reduce-scatter.42
  819.7 25.7 reduce-scatter.46
  887.6 25.3 reduce-scatter.44
  933.5 32.9 all-gather.35
  968.6 39.1 all-gather.49
  1010.0 25.4 reduce-scatter.30
  1037.6 25.7 reduce-scatter.48
  1103.6 25.3 reduce-scatter.50
  1184.9 29.9 all-gather.37
  1217.9 33.4 reduce-scatter.56
  1254.2 35.1 reduce-scatter.58
  1292.4 31.1 reduce-scatter.52
  1325.9 27.2 reduce-scatter.32
  (3 shorter events, 72.9 us)
